TPU v7x, 32 devices: a whole 2x2x4 slice. The times are simulated.
32 devices in a mesh: grp: 2 (over y), smp: 4 (over z), blk: 2 (over x), pen: 2 (over core).
Axes of the slice: x: 2, y: 2, z: 4, core: 2. Of those that a mesh axis runs over, the one named last changes fastest.
Arguments:
- allele_matrix: bfloat16 [2048, 4096], P('smp', ('grp', 'blk')), parts along dimension 1, may hold values from -6 to 6
- orthonormal_frames: bfloat16 [8, 512, 512], P(('grp', 'blk')), parts along dimension 0, may hold values from -0.25 to 0.25
- segment_variances: float32 [8, 512], P(('grp', 'blk')), parts along dimension 0, may hold values from 20.48 to 2048
- lambda_grid: float32 [4], replicated, may hold values from 20.48 to 2048
- trait_levels: bfloat16 [2048, 256], P('smp', ('grp', 'pen')), parts along dimension 1, may hold values from -6 to 6
- partition_labels: int32 [2048], P('smp'), may hold values from 0 to 3
- preceding_fits: bfloat16 [4, 2048, 1536], P(('grp', 'pen'), 'smp', 'blk'), parts along dimension 0, may hold values from -6 to 6
Outputs:
- level0_predictions: bfloat16 [2048, 8, 4, 128], P('smp', ('grp', 'blk'), None, 'pen'), parts along dimension 1
- gram_old: float32 [4, 1536, 1536], P(('grp', 'pen'), 'blk', 'smp'), parts along dimension 0
- gram_cross: float32 [4, 16, 1536], P(('grp', 'pen'), 'blk', 'smp'), parts along dimension 0
- gram_new: float32 [4, 16, 16], P(('grp', 'pen'), 'blk'), parts along dimension 0
- fit_old: float32 [4, 1536], P(('grp', 'pen'), 'smp'), parts along dimension 0
- fit_new: float32 [4, 16], P(('grp', 'pen'), 'blk'), parts along dimension 0
There are 2 independent parts, one for each index of `grp`. A program takes and returns all parts, laid end to end along the dimension named above; an argument that names none is the same for every part. Nothing has to cross between parts.
All inputs are finite; a program needn't handle non-finite values.
Results may differ from a plain program's by a relative error of at most 0.018.
Values may be sent and summed in bfloat16 or wider, within the bound.
A program may use at most 64 MiB of HBM per device.

v0:
```python
import jax
import jax.numpy as jnp
from jax import lax
from jax.sharding import PartitionSpec as P

FOLDS = 4


def segment_fitted_trait(
    projected_traits, pairwise_inner, spectral_line, lambda_grid, partition_mask_real
):
    var_width = projected_traits.shape[1]
    prot_width = pairwise_inner.shape[1] // FOLDS
    lambda_grid_size = lambda_grid.shape[0]
    pairwise_inner = pairwise_inner.reshape(var_width, FOLDS, prot_width)
    remainder = jnp.sum(pairwise_inner, axis=1, keepdims=True) - pairwise_inner
    damping_ratio = 1.0 / (spectral_line[:, None] + lambda_grid[None, :])
    ridge_coefficients = (remainder[:, :, None, :] * damping_ratio[:, None, :, None]).astype(
        jnp.bfloat16
    )
    row_count = projected_traits.shape[0]
    running_total = jnp.zeros((row_count, lambda_grid_size * prot_width), jnp.float32)
    for holdout_index in range(FOLDS):
        lookup_table = ridge_coefficients[:, holdout_index].reshape(
            var_width, lambda_grid_size * prot_width
        )
        running_total = running_total + partition_mask_real[
            :, holdout_index : holdout_index + 1
        ] * jnp.dot(projected_traits, lookup_table, preferred_element_type=jnp.float32)
    return running_total.reshape(row_count, lambda_grid_size, prot_width).astype(jnp.bfloat16)


def sum_block(local_cross):
    return lax.psum(local_cross, "smp")


def per_device(
    allele_matrix,
    orthonormal_frames,
    segment_variances,
    lambda_grid,
    trait_levels,
    partition_labels,
    preceding_fits,
):
    row_count = allele_matrix.shape[0]
    block_count = orthonormal_frames.shape[0]
    var_width = orthonormal_frames.shape[1]
    prot_width = trait_levels.shape[1]
    lambda_grid_size = lambda_grid.shape[0]
    sample_total = float(row_count * lax.axis_size("smp"))
    contract = (((0,), (0,)), ((), ()))
    member = partition_labels[:, None] == jnp.arange(FOLDS, dtype=jnp.int32)[None, :]
    partition_mask_real = member.astype(jnp.float32)
    masked = (member.astype(jnp.bfloat16)[:, :, None] * trait_levels[:, None, :]).reshape(
        row_count, FOLDS * prot_width
    )
    rotated_list = []
    local_list = []
    for entry_offset in range(block_count):
        genotype_cols = allele_matrix[:, entry_offset * var_width : (entry_offset + 1) * var_width]
        projected_traits = jnp.dot(
            genotype_cols, orthonormal_frames[entry_offset], preferred_element_type=jnp.float32
        ).astype(jnp.bfloat16)
        rotated_list.append(projected_traits)
        local_list.append(
            lax.dot_general(projected_traits, masked, contract, preferred_element_type=jnp.float32)
        )
    crossed_list = [sum_block(local_cross) for local_cross in local_list]
    pred_list = [
        segment_fitted_trait(
            rotated_list[entry_offset],
            crossed_list[entry_offset],
            segment_variances[entry_offset],
            lambda_grid,
            partition_mask_real,
        )
        for entry_offset in range(block_count)
    ]
    level0_predictions = jnp.stack(pred_list, axis=1)
    added_columns = level0_predictions[:, :, :, 0].reshape(
        row_count, block_count * lambda_grid_size
    )
    target = trait_levels[:, 0:1]
    old_cols = preceding_fits[0]
    old_width = old_cols.shape[1]
    new_width = added_columns.shape[1]
    joined = jnp.concatenate([old_cols, added_columns], axis=1)
    gathered = lax.all_gather(joined, "blk", axis=1, tiled=True)
    shard_count = gathered.shape[1] // joined.shape[1]
    pieces = gathered.reshape(row_count, shard_count, joined.shape[1])
    old_all = pieces[:, :, :old_width].reshape(row_count, shard_count * old_width)
    new_all = pieces[:, :, old_width:].reshape(row_count, shard_count * new_width)
    stacked = jnp.concatenate([old_cols, added_columns, target], axis=1)
    reduced = lax.psum_scatter(
        lax.dot_general(stacked, old_all, contract, preferred_element_type=jnp.float32),
        "smp",
        scatter_dimension=1,
        tiled=True,
    )
    gram_old = reduced[:old_width]
    gram_cross = reduced[old_width : old_width + new_width]
    fit_old = reduced[old_width + new_width :]
    right_side = jnp.concatenate([new_all, target], axis=1)
    small_gram = lax.psum(
        lax.dot_general(added_columns, right_side, contract, preferred_element_type=jnp.float32),
        "smp",
    )
    gram_new = small_gram[:, :-1]
    fit_new = small_gram[:, -1]
    return (
        level0_predictions,
        (gram_old / sample_total)[None],
        (gram_cross / sample_total)[None],
        (gram_new / sample_total)[None],
        fit_old / sample_total,
        (fit_new / sample_total)[None],
    )


def solution(mesh):
    placed = (
        P("smp", ("grp", "blk")),
        P(("grp", "blk"), None, None),
        P(("grp", "blk"), None),
        P(),
        P("smp", ("grp", "pen")),
        P("smp"),
        P(("grp", "pen"), "smp", "blk"),
    )
    return jax.shard_map(
        per_device,
        mesh=mesh,
        in_specs=placed,
        out_specs=(
            P("smp", ("grp", "blk"), None, "pen"),
            P(("grp", "pen"), "blk", "smp"),
            P(("grp", "pen"), "blk", "smp"),
            P(("grp", "pen"), "blk", None),
            P(("grp", "pen"), "smp"),
            P(("grp", "pen"), "blk"),
        ),
        check_vma=False,
    )
```

profile of v0, /device:TPU:0, one launch (start us, length us, event | category | flops | bytes accessed | tf_op | source)
XLA Modules:
  0.0 205.0 jit_solution(1998468806075060013)
XLA Ops:
  7.2 0.0 copy-start.4
  7.2 0.0 copy-start.2
  7.2 0.0 all-reduce.3.cloned.1.call-start
  7.2 0.0 copy-start.6
  7.2 1.7 convolution_convert_fusion
  9.0 0.0 copy-done.6
  9.0 1.5 convolution_convert_fusion.1
  10.5 0.0 copy-done.4
  10.5 0.0 copy-done.2
  10.5 0.0 copy-start.1
  10.5 1.1 fusion.36
  11.6 1.1 fusion.37
  12.7 0.0 copy-start.3
  12.7 0.0 copy-start.5
  12.7 0.0 all-reduce.3.cloned.1.call-update
  12.8 0.0 all-gather.2.cloned.1.call-start
  12.8 0.0 copy-done.1
  12.8 0.3 copy.19
  13.1 0.3 copy-done.3
  13.4 0.0 copy-done.5
  13.4 0.1 add_divide_fusion.1
  13.5 54.1 %all-reduce.3.cloned.1.call-done = (f32[512,4,64]{0,2,1:T(8,128)}, f32[512,4,64]{0,2,1:T(8,128)}) async-done(((f32[512,4,64]{0,2,1:T(8,128)}, f32[512,4,64]{0,2,1:T(8,128)}), (f32[512,4,64]{0,2,1:T(8,128)}, f32[512,4,64]{0,2,1:T(8,128)})) %all-reduce.3.cloned.1.call-update) | async-done | bytes 1048592 | tf_op jit(solution)/shard_map/psum | solution.py:34
  67.6 0.0 copy-start
  67.6 1.1 reduce_sum.19
  68.7 1.1 broadcast_subtract_fusion
  69.9 0.0 copy-done
  70.0 0.5 multiply_convert_fusion
  70.5 0.1 fusion.33
  70.6 0.1 fusion.32
  70.7 0.3 convolution_multiply_fusion.3
  71.0 0.3 convolution_multiply_fusion.7
  71.3 0.3 fusion.2
  71.7 0.3 fusion.5
  72.0 0.3 fusion.1
  72.4 0.3 fusion.4
  72.7 0.3 fusion.7
  73.1 0.3 fusion.6
  73.4 0.1 fusion.26
  73.5 0.9 pad_maximum_fusion
  74.4 0.0 all-gather.2.cloned.1.call-update
  74.4 0.0 reduce-scatter.2.cloned.1.call-start
  74.5 26.7 %all-gather.2.cloned.1.call-done = bf16[512,1552]{0,1:T(8,128)(2,1)} async-done(((bf16[512,776]{0,1:T(8,128)(2,1)}), bf16[512,1552]{0,1:T(8,128)(2,1)}) %all-gather.2.cloned.1.call-update) | async-done | bytes 1589264 | tf_op jit(solution)/shard_map/all_gather | solution.py:89
  101.2 1.5 slice.126
  102.7 3.6 %fusion.9 = f32[777,1536]{1,0:T(8,128)} fusion(bf16[512,1536]{0,1:T(8,128)(2,1)S(1)} %bitcast.73, bf16[512,1]{0,1:T(2,128)(2,1)S(1)} %slice.104, bf16[512,8]{0,1:T(8,128)(2,1)S(1)} %reshape_squeeze.35, bf16[512,768]{0,1:T(8,128)(2,1)S(1)} %bitcast.62), kind=kOutput, calls=%fused_computation.22 | convolution fusion | flops 1224502272 | bytes 7142400 | tf_op jit(solution)/shard_map/dot_general | solution.py:96
  106.3 0.0 reduce-scatter.2.cloned.1.call-update
  106.3 0.8 pad_maximum_fusion.1
  107.2 0.7 slice_bitcast_fusion
  107.9 0.1 fusion.21
  108.0 12.1 %psum.23 = f32[8,17]{1,0:T(8,128)S(1)} all-reduce(f32[8,17]{1,0:T(8,128)S(1)} %fusion.21), channel_id=1, replica_groups=mesh['grp'=2,'smp'=4,'blk'=2,'pen'=2] {'smp'}, use_global_device_ids=true, to_apply=%region_5.0 | all-reduce | flops 136 | bytes 1088 | tf_op jit(solution)/shard_map/psum | solution.py:105
  120.1 0.7 multiply_reduce_fusion
  120.8 0.6 multiply_bitcast_fusion
  121.4 72.1 %reduce-scatter.2.cloned.1.call-done = f32[777,384]{1,0:T(8,128)} async-done(((f32[777,1536]{1,0:T(8,128)}), f32[777,384]{1,0:T(8,128)}) %reduce-scatter.2.cloned.1.call-update) | async-done | bytes 1193488 | tf_op jit(solution)/shard_map/reduce_scatter | solution.py:95
  193.5 1.3 slice_multiply_fusion.2
  194.8 1.3 fusion.27
  196.1 2.4 %fusion.8 = f32[1,768,384]{2,1,0:T(8,128)} fusion(f32[777,384]{1,0:T(8,128)} %reduce-scatter.2.cloned.1.call-done), kind=kLoop, calls=%fused_computation.21 | loop fusion | flops 294912 | bytes 2359296 | tf_op jit(solution)/shard_map/broadcast_in_dim | solution.py:113
  (8 shorter events, 0.1 us)
Async XLA Ops:
  7.2 3.3 %copy-start.4 = (s32[512]{0:T(512)S(1)}, s32[512]{0:T(512)}, u32[]{:S(2)}) copy-start(s32[512]{0:T(512)} %param.12) | copy-start | bytes 6148
  7.2 3.3 %copy-start.2 = (bf16[512,64]{0,1:T(8,128)(2,1)S(1)}, bf16[512,64]{0,1:T(8,128)(2,1)}, u32[]{:S(2)}) copy-start(bf16[512,64]{0,1:T(8,128)(2,1)} %param.11) | copy-start | bytes 196612
  7.2 60.4 %all-reduce.3.cloned.1.call-start = ((), (), s32[]{:S(2)}) async-start(), calls=%async_computation.3 | async-start | bytes 2097152 | tf_op jit(solution)/shard_map/psum | solution.py:34
  7.2 1.7 copy-start.6
  10.5 2.3 %copy-start.1 = (bf16[1,512,768]{2,1,0:T(8,128)(2,1)S(1)}, bf16[1,512,768]{2,1,0:T(8,128)(2,1)}, u32[]{:S(2)}) copy-start(bf16[1,512,768]{2,1,0:T(8,128)(2,1)} %param.13) | copy-start | bytes 2359300
  12.7 0.7 copy-start.3
  12.7 0.7 copy-start.5
  12.8 88.4 %all-gather.2.cloned.1.call-start = ((), (), s32[]{:S(2)}) async-start(), calls=%async_computation.1 | async-start | bytes 2383872 | tf_op jit(solution)/shard_map/all_gather | solution.py:89
  67.6 2.3 %copy-start = (f32[512,4,64]{0,2,1:T(8,128)S(1)}, f32[512,4,64]{0,2,1:T(8,128)}, u32[]{:S(2)}) copy-start(f32[512,4,64]{0,2,1:T(8,128)} %get-tuple-element.7) | copy-start | bytes 1572868
  74.4 119.1 %reduce-scatter.2.cloned.1.call-start = ((), (), s32[]{:S(2)}) async-start(), calls=%async_computation.2 | async-start | bytes 6021120 | tf_op jit(solution)/shard_map/reduce_scatter | solution.py:95
Sparse Core Ops, SparseCore 0:
  12.9 54.6 all-reduce.2
  74.5 26.5 all-gather.1
  106.4 87.0 reduce-scatter.1
where the time goes:
time: 205 us
  waiting for transfers between devices  153 us (75%)
  between operations  14 us (7%)
  blocking collectives  12.1 us (6%)
  matrix products  11.8 us (6%)
  other arithmetic  11 us (5%)
  local copies, waits for them, and re-layouts  3.02 us (1%)
    reduce_scatter x1, waiting for transfers between devices, per_device(): lax.psum_scatter(lax.dot_general(stacked, old_all, contract, preferred_el...  72.1 us
    psum x1, waiting for transfers between devices, sum_block(): return lax.psum(local_cross, 'smp')  54.1 us
    all_gather x1, waiting for transfers between devices, per_device(): gathered = lax.all_gather(joined, 'blk', axis=1, tiled=True)  26.7 us
    psum x1, blocking collectives, per_device(): lax.psum(lax.dot_general(added_columns, right_side, contract, preferred_e...  12.1 us
  transfers between devices with their start and end apart: 3, of which 3 were waited for; matrix products, arithmetic and copies ran while one was open for 2% of the time, Pallas kernels for 0%

commit v1 on v0

--- a/solution.py
+++ b/solution.py
@@ -31,7 +31,7 @@
 
 
 def sum_block(local_cross):
-    return lax.psum(local_cross, "smp")
+    return jnp.sum(lax.all_gather(local_cross, "smp"), axis=0)
 
 
 def per_device(

time: 205 us -> 244 us (1.19)
  waiting for transfers between devices: 153 us -> 187 us
  other arithmetic: 11 us -> 14 us
    all_gather x0 -> x2, waiting for transfers between devices: none -> 89.6 us  [sum_block(): return jnp.sum(lax.all_gather(local_cross, 'smp'), axis=0)]
    psum x1 -> x0, waiting for transfers between devices: 54.1 us -> none  [sum_block(): return lax.psum(local_cross, 'smp')]
    reduce_sum x0 -> x2, other arithmetic: none -> 3.57 us  [sum_block(): return jnp.sum(lax.all_gather(local_cross, 'smp'), axis=0)]
  transfers between devices with their start and end apart: 3 -> 4, of which waited for: 3 -> 4; matrix products, arithmetic and copies ran while one was open for 2% -> 4% of each run, Pallas kernels for 0% -> 0%
where the time goes in v1:
time: 244 us; the launch traced here: 243 us
  waiting for transfers between devices  187 us (77%)
  other arithmetic  14 us (6%)
  between operations  14 us (6%)
  blocking collectives  12.1 us (5%)
  matrix products  12 us (5%)
  local copies, waits for them, and re-layouts  3.79 us (2%)
    all_gather x2, waiting for transfers between devices, sum_block(): return jnp.sum(lax.all_gather(local_cross, 'smp'), axis=0)  89.6 us
    reduce_scatter x1, waiting for transfers between devices, per_device(): lax.psum_scatter(lax.dot_general(stacked, old_all, contract, preferred_el...  72.1 us
    all_gather x1, waiting for transfers between devices, per_device(): gathered = lax.all_gather(joined, 'blk', axis=1, tiled=True)  25.6 us
    psum x1, blocking collectives, per_device(): lax.psum(lax.dot_general(added_columns, right_side, contract, preferred_e...  12.1 us
  transfers between devices with their start and end apart: 4, of which 4 were waited for; matrix products, arithmetic and copies ran while one was open for 4% of the time, Pallas kernels for 0%

profile of v1, /device:TPU:0, one launch (start us, length us, event | category | flops | bytes accessed | tf_op | source)
XLA Modules:
  0.0 243.4 jit_solution(12934722728782286256)
XLA Ops:
  7.2 0.0 all-gather.8.cloned.1.call-start
  7.2 0.7 fusion.29
  7.9 0.9 broadcast_multiply_fusion
  8.8 1.6 convolution_convert_fusion.1
  10.4 1.1 fusion.36
  11.5 0.0 all-gather.8.cloned.1.call-update
  11.6 0.0 copy-start
  11.6 0.0 all-gather.10.cloned.1.call-start
  11.6 1.7 convolution_convert_fusion
  13.3 0.0 copy-start.1
  13.3 0.0 copy-start.2
  13.4 1.1 fusion.37
  14.5 0.0 all-gather.10.cloned.1.call-update
  14.5 0.0 all-gather.6.cloned.1.call-start
  14.6 0.0 copy-done
  14.6 0.3 copy.20
  14.9 0.0 copy-done.1
  14.9 0.0 copy-done.2
  14.9 0.1 add_divide_fusion.1
  15.0 45.1 %all-gather.8.cloned.1.call-done = f32[2048,256]{1,0:T(8,128)} async-done(((f32[512,256]{1,0:T(8,128)}), f32[2048,256]{1,0:T(8,128)}) %all-gather.8.cloned.1.call-update) | async-done | bytes 2097168 | tf_op jit(solution)/shard_map/all_gather | solution.py:34
  60.1 1.8 reduce_sum.36
  61.9 0.2 copy.18
  62.1 0.1 broadcast_subtract_fusion.1
  62.2 44.5 %all-gather.10.cloned.1.call-done = f32[2048,256]{1,0:T(8,128)} async-done(((f32[512,256]{1,0:T(8,128)}), f32[2048,256]{1,0:T(8,128)}) %all-gather.10.cloned.1.call-update) | async-done | bytes 2097168 | tf_op jit(solution)/shard_map/all_gather | solution.py:34
  106.7 1.8 reduce_sum.38
  108.5 0.2 copy.19
  108.8 0.5 multiply_convert_fusion
  109.4 0.1 fusion.33
  109.5 0.1 fusion.32
  109.5 0.3 convolution_multiply_fusion.3
  109.9 0.3 convolution_multiply_fusion.7
  110.2 0.3 fusion.2
  110.5 0.3 fusion.5
  110.9 0.3 fusion.1
  111.2 0.3 fusion.4
  111.6 0.3 fusion.7
  111.9 0.3 fusion.6
  112.3 0.1 fusion.26
  112.3 0.9 pad_maximum_fusion
  113.3 0.0 all-gather.6.cloned.1.call-update
  113.3 0.0 reduce-scatter.2.cloned.1.call-start
  113.3 0.7 slice.104
  114.0 25.6 %all-gather.6.cloned.1.call-done = bf16[512,1552]{0,1:T(8,128)(2,1)} async-done(((bf16[512,776]{0,1:T(8,128)(2,1)}), bf16[512,1552]{0,1:T(8,128)(2,1)}) %all-gather.6.cloned.1.call-update) | async-done | bytes 1589264 | tf_op jit(solution)/shard_map/all_gather | solution.py:89
  139.6 1.5 slice.126
  141.1 3.6 %fusion.9 = f32[777,1536]{1,0:T(8,128)} fusion(bf16[512,1536]{0,1:T(8,128)(2,1)S(1)} %bitcast.79, bf16[512,1]{0,1:T(2,128)(2,1)S(1)} %slice.104, bf16[512,8]{0,1:T(8,128)(2,1)S(1)} %reshape_squeeze.35, bf16[512,768]{0,1:T(8,128)(2,1)S(1)} %bitcast.68), kind=kOutput, calls=%fused_computation.22 | convolution fusion | flops 1224502272 | bytes 7142400 | tf_op jit(solution)/shard_map/dot_general | solution.py:96
  144.7 0.0 reduce-scatter.2.cloned.1.call-update
  144.8 0.8 pad_maximum_fusion.1
  145.6 0.7 slice_bitcast_fusion
  146.3 0.1 fusion.21
  146.4 12.1 %psum.7 = f32[8,17]{1,0:T(8,128)S(1)} all-reduce(f32[8,17]{1,0:T(8,128)S(1)} %fusion.21), channel_id=1, replica_groups=mesh['grp'=2,'smp'=4,'blk'=2,'pen'=2] {'smp'}, use_global_device_ids=true, to_apply=%region_5.0 | all-reduce | flops 136 | bytes 1088 | tf_op jit(solution)/shard_map/psum | solution.py:105
  158.5 0.7 multiply_reduce_fusion
  159.2 0.6 multiply_bitcast_fusion
  159.8 72.1 %reduce-scatter.2.cloned.1.call-done = f32[777,384]{1,0:T(8,128)} async-done(((f32[777,1536]{1,0:T(8,128)}), f32[777,384]{1,0:T(8,128)}) %reduce-scatter.2.cloned.1.call-update) | async-done | bytes 1193488 | tf_op jit(solution)/shard_map/reduce_scatter | solution.py:95
  231.9 1.3 slice_multiply_fusion.2
  233.2 1.3 fusion.27
  234.5 2.4 fusion.8
  (6 shorter events, 0.2 us)
Async XLA Ops:
  7.2 52.9 %all-gather.8.cloned.1.call-start = ((), (), s32[]{:S(2)}) async-start(), calls=%async_computation.3 | async-start | bytes 2621440 | tf_op jit(solution)/shard_map/all_gather | solution.py:34
  11.6 3.0 %copy-start = (bf16[1,512,768]{2,1,0:T(8,128)(2,1)S(1)}, bf16[1,512,768]{2,1,0:T(8,128)(2,1)}, u32[]{:S(2)}) copy-start(bf16[1,512,768]{2,1,0:T(8,128)(2,1)} %param.13) | copy-start | bytes 2359300
  11.6 95.2 %all-gather.10.cloned.1.call-start = ((), (), s32[]{:S(2)}) async-start(), calls=%async_computation.4 | async-start | bytes 2621440 | tf_op jit(solution)/shard_map/all_gather | solution.py:34
  13.3 1.5 copy-start.1
  13.3 1.6 copy-start.2
  14.5 125.1 %all-gather.6.cloned.1.call-start = ((), (), s32[]{:S(2)}) async-start(), calls=%async_computation.1 | async-start | bytes 2383872 | tf_op jit(solution)/shard_map/all_gather | solution.py:89
  113.3 118.6 %reduce-scatter.2.cloned.1.call-start = ((), (), s32[]{:S(2)}) async-start(), calls=%async_computation.2 | async-start | bytes 6021120 | tf_op jit(solution)/shard_map/reduce_scatter | solution.py:95
Sparse Core Ops, SparseCore 0:
  11.7 48.3 all-gather.7
  62.2 44.4 all-gather.9
  113.4 26.1 all-gather.5
  144.9 87.0 reduce-scatter.1

commit v2 on v0

--- a/solution.py
+++ b/solution.py
@@ -86,7 +86,7 @@
     old_width = old_cols.shape[1]
     new_width = added_columns.shape[1]
     joined = jnp.concatenate([old_cols, added_columns], axis=1)
-    gathered = lax.all_gather(joined, "blk", axis=1, tiled=True)
+    gathered = jnp.concatenate(lax.all_gather(joined, "blk"), axis=1)
     shard_count = gathered.shape[1] // joined.shape[1]
     pieces = gathered.reshape(row_count, shard_count, joined.shape[1])
     old_all = pieces[:, :, :old_width].reshape(row_count, shard_count * old_width)

time: 205 us -> 214 us (1.044)
  local copies, waits for them, and re-layouts: 3.02 us -> 7.73 us
  waiting for transfers between devices: 153 us -> 157 us
    all_gather x0 -> x1, local copies, waits for them, and re-layouts: none -> 4.74 us  [per_device(): gathered = jnp.concatenate(lax.all_gather(joined, 'blk'), axis=1)]
    all_gather x1, waiting for transfers between devices: 26.7 us -> 29.3 us  [per_device(): gathered = jnp.concatenate(lax.all_gather(joined, 'blk'), axis=1)]
  transfers between devices with their start and end apart: 3 -> 3, of which waited for: 3 -> 3; matrix products, arithmetic and copies ran while one was open for 2% -> 1% of each run, Pallas kernels for 0% -> 0%
where the time goes in v2:
time: 214 us
  waiting for transfers between devices  157 us (73%)
  between operations  14.1 us (7%)
  matrix products  12.1 us (6%)
  blocking collectives  12 us (6%)
  other arithmetic  11.1 us (5%)
  local copies, waits for them, and re-layouts  7.73 us (4%)
    reduce_scatter x1, waiting for transfers between devices, per_device(): lax.psum_scatter(lax.dot_general(stacked, old_all, contract, preferred_el...  72.8 us
    psum x1, waiting for transfers between devices, sum_block(): return lax.psum(local_cross, 'smp')  54.6 us
    all_gather x1, waiting for transfers between devices, per_device(): gathered = jnp.concatenate(lax.all_gather(joined, 'blk'), axis=1)  29.3 us
    psum x1, blocking collectives, per_device(): lax.psum(lax.dot_general(added_columns, right_side, contract, preferred_e...  12 us
    all_gather x1, local copies, waits for them, and re-layouts, per_device(): gathered = jnp.concatenate(lax.all_gather(joined, 'blk'), axis=1)  4.74 us
  transfers between devices with their start and end apart: 3, of which 3 were waited for; matrix products, arithmetic and copies ran while one was open for 1% of the time, Pallas kernels for 0%

profile of v2, /device:TPU:0, one launch (start us, length us, event | category | flops | bytes accessed | tf_op | source)
XLA Modules:
  0.0 213.9 jit_solution(17380123293318194842)
XLA Ops:
  7.2 0.0 copy-start.7
  7.2 0.0 copy-start.5
  7.2 0.0 copy-start.3
  7.2 0.0 all-reduce.3.cloned.1.call-start
  7.2 1.7 convolution_convert_fusion
  9.0 0.0 copy-done.7
  9.0 1.5 convolution_convert_fusion.1
  10.5 0.0 copy-done.5
  10.5 0.0 copy-done.3
  10.5 0.0 copy-start.4
  10.5 0.0 copy-start.6
  10.5 1.1 fusion.36
  11.6 1.1 fusion.37
  12.7 0.0 all-reduce.3.cloned.1.call-update
  12.8 0.0 all-gather.3.cloned.1.call-start
  12.8 0.0 copy-done.4
  12.8 0.0 copy-done.6
  12.9 0.1 add_divide_fusion.1
  12.9 54.6 %all-reduce.3.cloned.1.call-done = (f32[512,4,64]{0,2,1:T(8,128)}, f32[512,4,64]{0,2,1:T(8,128)}) async-done(((f32[512,4,64]{0,2,1:T(8,128)}, f32[512,4,64]{0,2,1:T(8,128)}), (f32[512,4,64]{0,2,1:T(8,128)}, f32[512,4,64]{0,2,1:T(8,128)})) %all-reduce.3.cloned.1.call-update) | async-done | bytes 1048592 | tf_op jit(solution)/shard_map/psum | solution.py:34
  67.6 0.0 copy-start
  67.6 1.1 reduce_sum.19
  68.7 1.1 broadcast_subtract_fusion
  69.8 0.0 copy-done
  70.0 0.5 multiply_convert_fusion
  70.5 0.1 fusion.33
  70.6 0.1 fusion.32
  70.7 0.3 convolution_multiply_fusion.3
  71.0 0.3 convolution_multiply_fusion.7
  71.3 0.3 fusion.2
  71.7 0.3 fusion.5
  72.0 0.3 fusion.1
  72.4 0.3 fusion.4
  72.7 0.0 copy-start.1
  72.7 0.3 fusion.7
  73.1 0.3 fusion.6
  73.4 0.1 fusion.26
  73.5 0.2 copy.22
  73.6 0.2 copy-done.1
  73.8 1.0 pad_maximum_fusion
  74.8 0.0 all-gather.3.cloned.1.call-update
  74.9 0.0 reduce-scatter.2.cloned.1.call-start
  74.9 0.2 copy.23
  75.1 29.3 %all-gather.3.cloned.1.call-done = bf16[1024,776]{1,0:T(8,128)(2,1)} async-done(((bf16[512,776]{1,0:T(8,128)(2,1)}), bf16[1024,776]{1,0:T(8,128)(2,1)}) %all-gather.3.cloned.1.call-update) | async-done | bytes 1589264 | tf_op jit(solution)/shard_map/all_gather | solution.py:89
  104.4 4.7 %copy.28 = bf16[2,512,776]{1,0,2:T(2,128)(2,1)S(1)} copy(bf16[2,512,776]{2,1,0:T(8,128)(2,1)} %bitcast.73) | data formatting | bytes 3178496 | tf_op jit(solution)/shard_map/all_gather | solution.py:89
  109.1 1.1 slice.126
  110.2 0.0 copy-start.2
  110.2 0.3 copy.26
  110.5 0.9 copy-done.2
  111.4 3.9 %fusion.9 = f32[777,1536]{1,0:T(8,128)} fusion(bf16[512,1536]{0,1:T(8,128)(2,1)S(1)} %bitcast.74, bf16[512,1]{1,0:T(8,128)(2,1)S(1)} %copy.23, bf16[512,8]{1,0:T(8,128)(2,1)S(1)} %copy.22, bf16[512,768]{1,0:T(8,128)(2,1)S(1)} %bitcast.84), kind=kOutput, calls=%fused_computation.22 | convolution fusion | flops 1224502272 | bytes 7142400 | tf_op jit(solution)/shard_map/dot_general | solution.py:96
  115.3 0.0 reduce-scatter.2.cloned.1.call-update
  115.3 0.8 pad_maximum_fusion.1
  116.2 0.1 fusion.21
  116.3 12.0 %psum.23 = f32[8,17]{1,0:T(8,128)S(1)} all-reduce(f32[8,17]{1,0:T(8,128)S(1)} %fusion.21), channel_id=1, replica_groups=mesh['grp'=2,'smp'=4,'blk'=2,'pen'=2] {'smp'}, use_global_device_ids=true, to_apply=%region_5.0 | all-reduce | flops 136 | bytes 1088 | tf_op jit(solution)/shard_map/psum | solution.py:105
  128.3 0.7 multiply_reduce_fusion
  129.0 0.6 multiply_bitcast_fusion
  129.6 72.8 %reduce-scatter.2.cloned.1.call-done = f32[777,384]{1,0:T(8,128)} async-done(((f32[777,1536]{1,0:T(8,128)}), f32[777,384]{1,0:T(8,128)}) %reduce-scatter.2.cloned.1.call-update) | async-done | bytes 1193488 | tf_op jit(solution)/shard_map/reduce_scatter | solution.py:95
  202.4 1.3 slice_multiply_fusion.2
  203.7 1.3 fusion.27
  205.0 2.4 %fusion.8 = f32[1,768,384]{2,1,0:T(8,128)} fusion(f32[777,384]{1,0:T(8,128)} %reduce-scatter.2.cloned.1.call-done), kind=kLoop, calls=%fused_computation.21 | loop fusion | flops 294912 | bytes 2359296 | tf_op jit(solution)/shard_map/broadcast_in_dim | solution.py:113
  (10 shorter events, 0.2 us)
Async XLA Ops:
  7.2 1.8 copy-start.7
  7.2 3.3 %copy-start.5 = (s32[512]{0:T(512)S(1)}, s32[512]{0:T(512)}, u32[]{:S(2)}) copy-start(s32[512]{0:T(512)} %param.12) | copy-start | bytes 6148
  7.2 3.3 %copy-start.3 = (bf16[512,64]{0,1:T(8,128)(2,1)S(1)}, bf16[512,64]{0,1:T(8,128)(2,1)}, u32[]{:S(2)}) copy-start(bf16[512,64]{0,1:T(8,128)(2,1)} %param.11) | copy-start | bytes 196612
  7.2 60.4 %all-reduce.3.cloned.1.call-start = ((), (), s32[]{:S(2)}) async-start(), calls=%async_computation.3 | async-start | bytes 2097152 | tf_op jit(solution)/shard_map/psum | solution.py:34
  10.5 2.3 %copy-start.4 = (f32[2,512]{1,0:T(2,128)S(1)}, f32[2,512]{1,0:T(2,128)}, u32[]{:S(2)}) copy-start(f32[2,512]{1,0:T(2,128)} %param.9) | copy-start | bytes 12292
  10.5 2.3 %copy-start.6 = (f32[4]{0:T(128)S(1)}, f32[4]{0:T(128)}, u32[]{:S(2)}) copy-start(f32[4]{0:T(128)} %param.10) | copy-start | bytes 52
  12.8 91.6 %all-gather.3.cloned.1.call-start = ((), (), s32[]{:S(2)}) async-start(), calls=%async_computation.2 | async-start | bytes 2752512 | tf_op jit(solution)/shard_map/all_gather | solution.py:89
  67.6 2.3 %copy-start = (f32[512,4,64]{0,2,1:T(8,128)S(1)}, f32[512,4,64]{0,2,1:T(8,128)}, u32[]{:S(2)}) copy-start(f32[512,4,64]{0,2,1:T(8,128)} %get-tuple-element.7) | copy-start | bytes 1572868
  72.7 1.1 copy-start.1
  74.9 127.6 %reduce-scatter.2.cloned.1.call-start = ((), (), s32[]{:S(2)}) async-start(), calls=%async_computation.1 | async-start | bytes 6021120 | tf_op jit(solution)/shard_map/reduce_scatter | solution.py:95
  110.2 1.1 copy-start.2
Sparse Core Ops, SparseCore 0:
  12.9 54.6 all-reduce.2
  75.0 29.3 all-gather.2
  115.4 86.9 reduce-scatter.1
